TPU v7x, 32 devices: a whole 2x2x4 slice. The times are simulated.
32 devices in a mesh: dp: 16 (over z, x, core), tensor: 2 (over y).
Axes of the slice: x: 2, y: 2, z: 4, core: 2. Of those that a mesh axis runs over, the one named last changes fastest.
Arguments:
- tokens: bfloat16 [32768, 1024], P(('dp', 'tensor')), may hold values from -6 to 6
- w_qkv: bfloat16 [1024, 3, 1024], P('dp', None, 'tensor'), may hold values from -0.1875 to 0.1875
- w_out: bfloat16 [1024, 1024], P('tensor', 'dp'), may hold values from -0.75 to 0.75
- w_up: bfloat16 [1024, 4096], P('dp', 'tensor'), may hold values from -0.1875 to 0.1875
- w_down: bfloat16 [4096, 1024], P('tensor', 'dp'), may hold values from -0.09375 to 0.09375
- ln1_gain: float32 [1024], replicated, may hold values from 0.5 to 1.5
- ln1_bias: float32 [1024], replicated, may hold values from -1.5 to 1.5
- ln2_gain: float32 [1024], replicated, may hold values from 0.5 to 1.5
- ln2_bias: float32 [1024], replicated, may hold values from -1.5 to 1.5
- a_qkv: bfloat16 [8, 1024, 16], replicated, may hold values from -0.1875 to 0.1875
- b_qkv: bfloat16 [8, 16, 3, 1024], P(None, None, None, 'tensor'), may hold values from -0.75 to 0.75
- a_out: bfloat16 [8, 1024, 16], P(None, 'tensor'), may hold values from -0.75 to 0.75
- b_out: bfloat16 [8, 16, 1024], replicated, may hold values from -0.75 to 0.75
- a_up: bfloat16 [8, 1024, 16], replicated, may hold values from -0.1875 to 0.1875
- b_up: bfloat16 [8, 16, 4096], P(None, None, 'tensor'), may hold values from -0.75 to 0.75
- a_down: bfloat16 [8, 4096, 16], P(None, 'tensor'), may hold values from -0.09375 to 0.09375
- b_down: bfloat16 [8, 16, 1024], replicated, may hold values from -0.75 to 0.75
- adapter_idx: int32 [16, 4], P('dp'), may hold values from 0 to 7
- pic_start: int32 [16, 2], P('dp'), may hold values from 0 to 1792, as said below
- cotangent: bfloat16 [32768, 1024], P(('dp', 'tensor')), may hold values from -6 to 6
Outputs:
- layer_out: bfloat16 [32768, 1024], P(('dp', 'tensor'))
- grad_tokens: float32 [32768, 1024], P(('dp', 'tensor'))
- grad_a_qkv: float32 [8, 1024, 16], replicated
- grad_b_qkv: float32 [8, 16, 3, 1024], P(None, None, None, 'tensor')
- grad_a_out: float32 [8, 1024, 16], P(None, 'tensor')
- grad_b_out: float32 [8, 16, 1024], replicated
- grad_a_up: float32 [8, 1024, 16], replicated
- grad_b_up: float32 [8, 16, 4096], P(None, None, 'tensor')
- grad_a_down: float32 [8, 4096, 16], P(None, 'tensor')
- grad_b_down: float32 [8, 16, 1024], replicated
Inputs may be any that keep to these rules, and one draw needn't show every extreme that they name: `pic_start`: each sequence has 2 picture spans of 256 tokens; span k starts between k * 1024 and (k + 1) * 1024 - 256, so spans never intersect.
All inputs are finite; a program needn't handle non-finite values.
Results may differ from a plain program's by a relative error of at most 0.014.
Values may be sent and summed in bfloat16 or wider, within the bound.
A program may use at most 320 MiB of HBM per device.

v0:
```python
import jax
import jax.numpy as jnp
from jax import lax
from jax.sharding import PartitionSpec as P

HD = 64
SPAN = 256
BLOCK = 512


def matmul(left, right):
    return jnp.dot(left, right, preferred_element_type=jnp.float32)


def contract_rows(left, right):
    return lax.dot_general(
        left, right, (((0,), (0,)), ((), ())), preferred_element_type=jnp.float32
    )


def against(left, right):
    return lax.dot_general(
        left, right, (((1,), (1,)), ((), ())), preferred_element_type=jnp.float32
    )


def layer_norm(values, multiplier, addend):
    center = values - jnp.mean(values, axis=-1, keepdims=True)
    spread = jnp.mean(center * center, axis=-1, keepdims=True)
    return center * lax.rsqrt(spread + 1e-05) * multiplier + addend


def span_labels(positions, starts):
    inside = (positions[:, None] >= starts[None, :]) & (positions[:, None] < starts[None, :] + SPAN)
    labels = jnp.arange(1, starts.shape[0] + 1, dtype=jnp.int32)
    return jnp.sum(jnp.where(inside, labels[None, :], 0), axis=1)


def allowed_mask(offset, row_count, length, starts):
    row_pos = offset + jnp.arange(row_count, dtype=jnp.int32)
    col_pos = jnp.arange(length, dtype=jnp.int32)
    row_span = span_labels(row_pos, starts)
    col_span = span_labels(col_pos, starts)
    causal = col_pos[None, :] <= row_pos[:, None]
    joined = (row_span[:, None] == col_span[None, :]) & (row_span[:, None] > 0)
    return causal | joined


def masked_scores(query_block, key_rows, offset, length, starts, factor):
    scores = (
        jnp.einsum("qhd,khd->hqk", query_block, key_rows, preferred_element_type=jnp.float32)
        * factor
    )
    allowed = allowed_mask(offset, BLOCK, length, starts)
    return jnp.where(allowed[None], scores, -1000000000.0)


def attend(queries, key_rows, value_rows, starts):
    length, heads, width = queries.shape
    factor = width ** (-0.5)

    def one_block(block_number):
        offset = block_number * BLOCK
        query_block = lax.dynamic_slice_in_dim(queries, offset, BLOCK, 0)
        scores = masked_scores(query_block, key_rows, offset, length, starts, factor)
        peak = jnp.max(scores, axis=-1, keepdims=True)
        raised = jnp.exp(scores - peak)
        totals = jnp.sum(raised, axis=-1, keepdims=True)
        weights_low = (raised / totals).astype(jnp.bfloat16)
        blended = jnp.einsum(
            "hqk,khd->qhd", weights_low, value_rows, preferred_element_type=jnp.float32
        )
        return (
            blended.astype(jnp.bfloat16).reshape(BLOCK, heads * width),
            (peak + jnp.log(totals))[..., 0],
        )

    blended, log_sums = lax.map(one_block, jnp.arange(length // BLOCK, dtype=jnp.int32))
    return (blended.reshape(length, heads * width), log_sums)


def attend_back(queries, key_rows, value_rows, grad_mix, log_sums, starts):
    length, heads, width = queries.shape
    factor = width ** (-0.5)

    def one_block(carry, inputs_pair):
        key_grad, value_grad = carry
        block_number, block_sums = inputs_pair
        offset = block_number * BLOCK
        query_block = lax.dynamic_slice_in_dim(queries, offset, BLOCK, 0)
        grad_block = lax.dynamic_slice_in_dim(grad_mix, offset, BLOCK, 0)
        scores = masked_scores(query_block, key_rows, offset, length, starts, factor)
        weights = jnp.exp(scores - block_sums[:, :, None])
        dots = jnp.einsum(
            "qhd,khd->hqk", grad_block, value_rows, preferred_element_type=jnp.float32
        )
        inner = jnp.sum(weights * dots, axis=-1, keepdims=True)
        slopes = (weights * (dots - inner) * factor).astype(jnp.bfloat16)
        query_grad = jnp.einsum(
            "hqk,khd->qhd", slopes, key_rows, preferred_element_type=jnp.float32
        )
        key_grad = key_grad + jnp.einsum(
            "hqk,qhd->khd", slopes, query_block, preferred_element_type=jnp.float32
        )
        value_grad = value_grad + jnp.einsum(
            "hqk,qhd->khd",
            weights.astype(jnp.bfloat16),
            grad_block,
            preferred_element_type=jnp.float32,
        )
        return ((key_grad, value_grad), query_grad)

    initial = jnp.zeros(key_rows.shape, jnp.float32)
    numbers = jnp.arange(length // BLOCK, dtype=jnp.int32)
    (key_grad, value_grad), query_grad = lax.scan(
        one_block, (initial, initial), (numbers, log_sums)
    )
    return (query_grad.reshape(length, heads, width), key_grad, value_grad)


def fetch_frozen(first, second):
    return (
        lax.all_gather(first, "dp", axis=0, tiled=True),
        lax.all_gather(second, "dp", axis=1, tiled=True),
    )


def enter_rows(normed, reduced):
    return (
        lax.all_gather(normed, "tensor", axis=0, tiled=True),
        lax.all_gather(reduced, "tensor", axis=0, tiled=True),
    )


def leave_rows(partial_value, reduced):
    return (
        lax.psum_scatter(partial_value, "tensor", scatter_dimension=0, tiled=True),
        lax.psum_scatter(reduced, "tensor", scatter_dimension=0, tiled=True),
    )


def enter_grads(branch, reduced):
    return (
        lax.all_gather(branch, "tensor", axis=0, tiled=True),
        lax.all_gather(reduced, "tensor", axis=0, tiled=True),
    )


def leave_grads(partial_value, reduced):
    return (
        lax.psum_scatter(partial_value, "tensor", scatter_dimension=0, tiled=True),
        lax.psum_scatter(reduced, "tensor", scatter_dimension=0, tiled=True),
    )


def per_device(
    tokens,
    w_qkv,
    w_out,
    w_up,
    w_down,
    ln1_gain,
    ln1_bias,
    ln2_gain,
    ln2_bias,
    a_qkv,
    b_qkv,
    a_out,
    b_out,
    a_up,
    b_up,
    a_down,
    b_down,
    adapter_idx,
    pic_start,
    cotangent,
):
    selection = adapter_idx[0]
    starts = pic_start[0]

    def chosen(stacked, which_one):
        return lax.dynamic_index_in_dim(stacked, selection[which_one], 0, keepdims=False)

    low_qkv_in = chosen(a_qkv, 0)
    rank = low_qkv_in.shape[1]
    low_qkv_out = chosen(b_qkv, 0).reshape(rank, -1)
    low_out_in = chosen(a_out, 1)
    low_out_out = chosen(b_out, 1)
    low_up_in = chosen(a_up, 2)
    low_up_out = chosen(b_up, 2)
    low_down_in = chosen(a_down, 3)
    low_down_out = chosen(b_down, 3)
    heads_here = low_out_in.shape[0] // HD

    def run_forward(own_tokens, frozen):
        qkv_rows, out_rows, up_rows, down_rows = frozen
        qkv_full, out_full = fetch_frozen(qkv_rows, out_rows)
        qkv_flat = qkv_full.reshape(qkv_full.shape[0], -1)
        own_float = own_tokens.astype(jnp.float32)
        normed = layer_norm(own_float, ln1_gain, ln1_bias).astype(jnp.bfloat16)
        reduced = matmul(normed, low_qkv_in).astype(jnp.bfloat16)
        normed_all, reduced_all = enter_rows(normed, reduced)
        length = normed_all.shape[0]
        project = (matmul(normed_all, qkv_flat) + matmul(reduced_all, low_qkv_out)).astype(
            jnp.bfloat16
        )
        split = project.reshape(length, 3, heads_here, HD)
        blended, log_sums = attend(split[:, 0], split[:, 1], split[:, 2], starts)
        main_part, low_part = leave_rows(matmul(blended, out_full), matmul(blended, low_out_in))
        low_out_val = low_part.astype(jnp.bfloat16)
        residual = own_float + main_part + matmul(low_out_val, low_out_out)
        up_full, down_full = fetch_frozen(up_rows, down_rows)
        normed_two = layer_norm(residual, ln2_gain, ln2_bias).astype(jnp.bfloat16)
        reduced_two = matmul(normed_two, low_up_in).astype(jnp.bfloat16)
        normed_two_all, reduced_two_all = enter_rows(normed_two, reduced_two)
        pre_act = matmul(normed_two_all, up_full) + matmul(reduced_two_all, low_up_out)
        hidden = jax.nn.gelu(pre_act, approximate=True).astype(jnp.bfloat16)
        main_two, low_two = leave_rows(matmul(hidden, down_full), matmul(hidden, low_down_in))
        low_down_val = low_two.astype(jnp.bfloat16)
        output = residual + main_two + matmul(low_down_val, low_down_out)
        kept_state = (
            qkv_flat,
            out_full,
            up_full,
            down_full,
            normed,
            reduced_all,
            split,
            blended,
            log_sums,
            low_out_val,
            residual,
            normed_two,
            reduced_two_all,
            pre_act,
            hidden,
            low_down_val,
        )
        return (output, kept_state)

    frozen = (w_qkv, w_out, w_up, w_down)
    output, kept_state = run_forward(tokens, frozen)
    fresh_tokens, fresh_frozen = lax.optimization_barrier((tokens, frozen))
    repeat_out, kept_state = run_forward(fresh_tokens, fresh_frozen)
    (
        qkv_flat,
        out_full,
        up_full,
        down_full,
        normed,
        reduced_all,
        split,
        blended,
        log_sums,
        low_out_val,
        residual,
        normed_two,
        reduced_two_all,
        pre_act,
        hidden,
        low_down_val,
    ) = kept_state
    cot_float = cotangent.astype(jnp.float32)
    grad_low_down = against(cotangent, low_down_out).astype(jnp.bfloat16)
    grad_b_down_here = contract_rows(low_down_val, cotangent)
    cot_all, grad_low_down_all = enter_grads(cotangent, grad_low_down)
    grad_hidden = against(cot_all, down_full) + against(grad_low_down_all, low_down_in)
    grad_a_down_here = contract_rows(hidden, grad_low_down_all)
    gelu_pull = jax.vjp(lambda inner_val: jax.nn.gelu(inner_val, approximate=True), pre_act)[1]
    grad_pre = gelu_pull(grad_hidden)[0].astype(jnp.bfloat16)
    grad_b_up_here = contract_rows(reduced_two_all, grad_pre)
    grad_normed_two, grad_reduced_two = leave_grads(
        against(grad_pre, up_full), against(grad_pre, low_up_out)
    )
    grad_low_up = grad_reduced_two.astype(jnp.bfloat16)
    grad_a_up_here = contract_rows(normed_two, grad_low_up)
    grad_normed_two = grad_normed_two + against(grad_low_up, low_up_in)
    norm_pull_two = jax.vjp(lambda inner_val: layer_norm(inner_val, ln2_gain, ln2_bias), residual)[
        1
    ]
    grad_resid = cot_float + norm_pull_two(grad_normed_two)[0]
    branch_low = grad_resid.astype(jnp.bfloat16)
    grad_low_out = against(branch_low, low_out_out).astype(jnp.bfloat16)
    grad_b_out_here = contract_rows(low_out_val, branch_low)
    branch_all, grad_low_out_all = enter_grads(branch_low, grad_low_out)
    grad_mix = (against(branch_all, out_full) + against(grad_low_out_all, low_out_in)).astype(
        jnp.bfloat16
    )
    grad_a_out_here = contract_rows(blended, grad_low_out_all)
    length = grad_mix.shape[0]
    query_grad, key_grad, value_grad = attend_back(
        split[:, 0],
        split[:, 1],
        split[:, 2],
        grad_mix.reshape(length, heads_here, HD),
        log_sums,
        starts,
    )
    grad_qkv = (
        jnp.stack([query_grad, key_grad, value_grad], axis=1)
        .reshape(length, -1)
        .astype(jnp.bfloat16)
    )
    grad_b_qkv_here = contract_rows(reduced_all, grad_qkv)
    grad_normed_one, grad_reduced_one = leave_grads(
        against(grad_qkv, qkv_flat), against(grad_qkv, low_qkv_out)
    )
    grad_low_qkv = grad_reduced_one.astype(jnp.bfloat16)
    grad_a_qkv_here = contract_rows(normed, grad_low_qkv)
    grad_normed_one = grad_normed_one + against(grad_low_qkv, low_qkv_in)
    norm_pull_one = jax.vjp(
        lambda inner_val: layer_norm(inner_val, ln1_gain, ln1_bias), tokens.astype(jnp.float32)
    )[1]
    grad_input = grad_resid + norm_pull_one(grad_normed_one)[0]
    slots = a_qkv.shape[0]

    def spread(gradient, which_one):
        onehot = (jnp.arange(slots, dtype=jnp.int32) == selection[which_one]).astype(jnp.float32)
        return onehot.reshape((slots,) + (1,) * gradient.ndim) * gradient[None]

    sharded = (
        lax.psum(spread(grad_b_qkv_here.reshape(rank, 3, -1), 0).astype(jnp.bfloat16), "dp").astype(
            jnp.float32
        ),
        lax.psum(spread(grad_a_out_here, 1).astype(jnp.bfloat16), "dp").astype(jnp.float32),
        lax.psum(spread(grad_b_up_here, 2).astype(jnp.bfloat16), "dp").astype(jnp.float32),
        lax.psum(spread(grad_a_down_here, 3).astype(jnp.bfloat16), "dp").astype(jnp.float32),
    )
    shared = lax.psum(
        (
            spread(grad_a_qkv_here, 0),
            spread(grad_b_out_here, 1),
            spread(grad_a_up_here, 2),
            spread(grad_b_down_here, 3),
        ),
        ("dp", "tensor"),
    )
    return (
        output.astype(jnp.bfloat16),
        grad_input,
        shared[0],
        sharded[0],
        sharded[1],
        shared[1],
        shared[2],
        sharded[2],
        sharded[3],
        shared[3],
    )


def solution(mesh):
    placed = (
        P(("dp", "tensor"), None),
        P("dp", None, "tensor"),
        P("tensor", "dp"),
        P("dp", "tensor"),
        P("tensor", "dp"),
        P(),
        P(),
        P(),
        P(),
        P(),
        P(None, None, None, "tensor"),
        P(None, "tensor", None),
        P(),
        P(),
        P(None, None, "tensor"),
        P(None, "tensor", None),
        P(),
        P("dp", None),
        P("dp", None),
        P(("dp", "tensor"), None),
    )
    return jax.shard_map(
        per_device,
        mesh=mesh,
        in_specs=placed,
        out_specs=(
            P(("dp", "tensor"), None),
            P(("dp", "tensor"), None),
            P(),
            P(None, None, None, "tensor"),
            P(None, "tensor", None),
            P(),
            P(),
            P(None, None, "tensor"),
            P(None, "tensor", None),
            P(),
        ),
        check_vma=False,
    )
```

profile of v0, /device:TPU:0, one launch (start us, length us, event | category | flops | bytes accessed | tf_op | source)
XLA Modules:
  0.0 2569.9 jit_solution(11967599070437223480)
XLA Ops:
  63.1 52.4 %all-gather.31.cloned.1.call-done = bf16[2048,1024]{1,0:T(8,128)(2,1)} async-done(((bf16[1024,1024]{1,0:T(8,128)(2,1)}), bf16[2048,1024]{1,0:T(8,128)(2,1)}) %all-gather.31.cloned.1.call-update) | async-done | bytes 4194320 | tf_op jit(solution)/shard_map/all_gather | solution.py:130
  131.2 196.8 %while.38 = (s32[]{:T(128)}, bf16[4,512,512]{2,1,0:T(8,128)(2,1)}, f32[4,8,512]{2,1,0:T(8,128)S(1)}, s32[4]{0:T(128)S(1)}, s32[1,2]{1,0:T(1,128)S(1)}, /*index=5...) while((s32[]{:T(128)}, bf16[4,512,512]{2,1,0:T(8,128)(2,1)}, ...), condition=%wide.region_21.22_spmd, body=%wide.region_16.21_spmd.sunk | while | flops 2252623360 | bytes 112358664 | solution.py:78
  341.6 101.4 %reduce-scatter.20.cloned.1.call-done = f32[1024,1024]{1,0:T(8,128)} async-done(((f32[2048,1024]{1,0:T(8,128)}), f32[1024,1024]{1,0:T(8,128)}) %reduce-scatter.20.cloned.1.call-update) | async-done | bytes 4194320 | tf_op jit(solution)/shard_map/reduce_scatter | solution.py:137
  496.0 56.9 %all-gather.37.cloned.1.call-done = bf16[2048,1024]{1,0:T(8,128)(2,1)} async-done(((bf16[1024,1024]{1,0:T(8,128)(2,1)}), bf16[2048,1024]{1,0:T(8,128)(2,1)}) %all-gather.37.cloned.1.call-update) | async-done | bytes 4194320 | tf_op jit(solution)/shard_map/all_gather | solution.py:130
  611.2 53.0 %all-gather.27.cloned.1.call-done = bf16[2048,1024]{0,1:T(8,128)(2,1)} async-done(((bf16[2048,64]{0,1:T(8,128)(2,1)}), bf16[2048,1024]{0,1:T(8,128)(2,1)}) %all-gather.27.cloned.1.call-update) | async-done | bytes 4194320 | tf_op jit(solution)/shard_map/all_gather | solution.py:124
  709.8 97.8 %reduce-scatter.24.cloned.1.call-done = f32[1024,1024]{1,0:T(8,128)} async-done(((f32[2048,1024]{1,0:T(8,128)}), f32[1024,1024]{1,0:T(8,128)}) %reduce-scatter.24.cloned.1.call-update) | async-done | bytes 4194320 | tf_op jit(solution)/shard_map/reduce_scatter | solution.py:151
  825.0 49.9 %all-gather.41.cloned.1.call-done = bf16[2048,1024]{1,0:T(8,128)(2,1)} async-done(((bf16[1024,1024]{1,0:T(8,128)(2,1)}), bf16[2048,1024]{1,0:T(8,128)(2,1)}) %all-gather.41.cloned.1.call-update) | async-done | bytes 4194320 | tf_op jit(solution)/shard_map/all_gather | solution.py:144
  882.6 636.9 %while.39 = (s32[]{:T(128)}, f32[2048,8,64]{0,2,1:T(8,128)}, f32[2048,8,64]{0,2,1:T(8,128)}, bf16[4,512,8,64]{1,0,3,2:T(4,128)(2,1)}, s32[4]{0:T(128)S(1)}, /*in...) while((s32[]{:T(128)}, f32[2048,8,64]{0,2,1:T(8,128)}, ...), condition=%wide.region_34.35_spmd.clone, body=%wide.region_30.34_spmd.clone.sunk | while | flops 5494574592 | bytes 331953440 | solution.py:115
  932.6 42.6 %fusion.336 = bf16[1,512,8,64]{1,3,2,0:T(8,128)(2,1)S(1)} fusion(bf16[2048,8,64]{0,2,1:T(8,128)(2,1)} %get-tuple-element.550, f32[8,512,2048]{2,1,0:T(8,128)} %subtract_exponential_fusion.4, f32[8,512,2048]{2,1,0:T(8,128)} %fusion.335), kind=kOutput, calls=%fused_computation.66.clone.1 | convolution fusion | flops 1115691008 | bytes 69730304 | tf_op jit(solution)/shard_map/while/body/eval_jaxpr/hqk,khd->qhd/dot_general | solution.py:99
  975.2 43.4 %bitcast_add_fusion.5 = f32[2048,8,64]{0,2,1:T(8,128)} fusion(f32[2048,8,64]{0,2,1:T(8,128)} %get-tuple-element.529, f32[8,512,2048]{2,1,0:T(8,128)} %subtract_exponential_fusion.4, f32[8,512,2048]{2,1,0:T(8,128)} %fusion.335, pred[]{:T(512)S(6)} %compare.3, bf16[2048,8,64]{0,2,1:T(8,128)(2,1)} %get-tuple-element.548, s32[]{:T(128)S(6)} %select_n.138), kind=kOutput, calls=%fused_computation.63.clone.1 | convolution fusion | flops 1117788160 | bytes 143130624 | tf_op jit(solution)/shard_map/while/body/eval_jaxpr/hqk,qhd->khd/dot_general | solution.py:102
  1091.2 42.6 %fusion.336 = bf16[1,512,8,64]{1,3,2,0:T(8,128)(2,1)S(1)} fusion(bf16[2048,8,64]{0,2,1:T(8,128)(2,1)} %get-tuple-element.550, f32[8,512,2048]{2,1,0:T(8,128)} %subtract_exponential_fusion.4, f32[8,512,2048]{2,1,0:T(8,128)} %fusion.335), kind=kOutput, calls=%fused_computation.66.clone.1 | convolution fusion | flops 1115691008 | bytes 69730304 | tf_op jit(solution)/shard_map/while/body/eval_jaxpr/hqk,khd->qhd/dot_general | solution.py:99
  1133.7 44.6 %bitcast_add_fusion.5 = f32[2048,8,64]{0,2,1:T(8,128)} fusion(f32[2048,8,64]{0,2,1:T(8,128)} %get-tuple-element.529, f32[8,512,2048]{2,1,0:T(8,128)} %subtract_exponential_fusion.4, f32[8,512,2048]{2,1,0:T(8,128)} %fusion.335, pred[]{:T(512)S(6)} %compare.3, bf16[2048,8,64]{0,2,1:T(8,128)(2,1)} %get-tuple-element.548, s32[]{:T(128)S(6)} %select_n.138), kind=kOutput, calls=%fused_computation.63.clone.1 | convolution fusion | flops 1117788160 | bytes 143130624 | tf_op jit(solution)/shard_map/while/body/eval_jaxpr/hqk,qhd->khd/dot_general | solution.py:102
  1250.9 42.6 %fusion.336 = bf16[1,512,8,64]{1,3,2,0:T(8,128)(2,1)S(1)} fusion(bf16[2048,8,64]{0,2,1:T(8,128)(2,1)} %get-tuple-element.550, f32[8,512,2048]{2,1,0:T(8,128)} %subtract_exponential_fusion.4, f32[8,512,2048]{2,1,0:T(8,128)} %fusion.335), kind=kOutput, calls=%fused_computation.66.clone.1 | convolution fusion | flops 1115691008 | bytes 69730304 | tf_op jit(solution)/shard_map/while/body/eval_jaxpr/hqk,khd->qhd/dot_general | solution.py:99
  1293.4 44.6 %bitcast_add_fusion.5 = f32[2048,8,64]{0,2,1:T(8,128)} fusion(f32[2048,8,64]{0,2,1:T(8,128)} %get-tuple-element.529, f32[8,512,2048]{2,1,0:T(8,128)} %subtract_exponential_fusion.4, f32[8,512,2048]{2,1,0:T(8,128)} %fusion.335, pred[]{:T(512)S(6)} %compare.3, bf16[2048,8,64]{0,2,1:T(8,128)(2,1)} %get-tuple-element.548, s32[]{:T(128)S(6)} %select_n.138), kind=kOutput, calls=%fused_computation.63.clone.1 | convolution fusion | flops 1117788160 | bytes 143130624 | tf_op jit(solution)/shard_map/while/body/eval_jaxpr/hqk,qhd->khd/dot_general | solution.py:102
  1410.7 42.6 %fusion.336 = bf16[1,512,8,64]{1,3,2,0:T(8,128)(2,1)S(1)} fusion(bf16[2048,8,64]{0,2,1:T(8,128)(2,1)} %get-tuple-element.550, f32[8,512,2048]{2,1,0:T(8,128)} %subtract_exponential_fusion.4, f32[8,512,2048]{2,1,0:T(8,128)} %fusion.335), kind=kOutput, calls=%fused_computation.66.clone.1 | convolution fusion | flops 1115691008 | bytes 69730304 | tf_op jit(solution)/shard_map/while/body/eval_jaxpr/hqk,khd->qhd/dot_general | solution.py:99
  1453.3 44.6 %bitcast_add_fusion.5 = f32[2048,8,64]{0,2,1:T(8,128)} fusion(f32[2048,8,64]{0,2,1:T(8,128)} %get-tuple-element.529, f32[8,512,2048]{2,1,0:T(8,128)} %subtract_exponential_fusion.4, f32[8,512,2048]{2,1,0:T(8,128)} %fusion.335, pred[]{:T(512)S(6)} %compare.3, bf16[2048,8,64]{0,2,1:T(8,128)(2,1)} %get-tuple-element.548, s32[]{:T(128)S(6)} %select_n.138), kind=kOutput, calls=%fused_computation.63.clone.1 | convolution fusion | flops 1117788160 | bytes 143130624 | tf_op jit(solution)/shard_map/while/body/eval_jaxpr/hqk,qhd->khd/dot_general | solution.py:102
  1545.5 98.0 %reduce-scatter.28.cloned.1.call-done = f32[1024,1024]{1,0:T(8,128)} async-done(((f32[2048,1024]{1,0:T(8,128)}), f32[1024,1024]{1,0:T(8,128)}) %reduce-scatter.28.cloned.1.call-update) | async-done | bytes 4194320 | tf_op jit(solution)/shard_map/reduce_scatter | solution.py:151
  1701.6 47.1 %all-gather.15.cloned.1.call-done = bf16[2048,1024]{1,0:T(8,128)(2,1)} async-done(((bf16[1024,1024]{1,0:T(8,128)(2,1)}), bf16[2048,1024]{1,0:T(8,128)(2,1)}) %all-gather.15.cloned.1.call-update) | async-done | bytes 4194320 | tf_op jit(solution)/shard_map/all_gather | solution.py:130
  1764.3 144.6 %while.37 = (s32[]{:T(128)}, bf16[4,512,512]{2,1,0:T(8,128)(2,1)}, s32[4]{0:T(128)S(1)}, s32[1,2]{1,0:T(1,128)S(1)}, bf16[2048,8,64]{0,2,1:T(8,128)(2,1)}, /*ind...) while((s32[]{:T(128)}, bf16[4,512,512]{2,1,0:T(8,128)(2,1)}, ...), condition=%wide.region_7.8_spmd, body=%wide.region_2.7_spmd.sunk | while | flops 2202297856 | bytes 76608768 | solution.py:78
  1922.2 101.7 %reduce-scatter.12.cloned.1.call-done = f32[1024,1024]{1,0:T(8,128)} async-done(((f32[2048,1024]{1,0:T(8,128)}), f32[1024,1024]{1,0:T(8,128)}) %reduce-scatter.12.cloned.1.call-update) | async-done | bytes 4194320 | tf_op jit(solution)/shard_map/reduce_scatter | solution.py:137
  2076.5 57.3 %all-gather.21.cloned.1.call-done = bf16[2048,1024]{1,0:T(8,128)(2,1)} async-done(((bf16[1024,1024]{1,0:T(8,128)(2,1)}), bf16[2048,1024]{1,0:T(8,128)(2,1)}) %all-gather.21.cloned.1.call-update) | async-done | bytes 4194320 | tf_op jit(solution)/shard_map/all_gather | solution.py:130
  2210.7 88.6 %all-reduce.7.cloned.1.call-done = (bf16[8,16,3,512]{3,1,2,0:T(8,128)(2,1)}, bf16[8,512,16]{1,2,0:T(8,128)(2,1)}, bf16[8,16,2048]{2,1,0:T(8,128)(2,1)}, bf16[8,2048,16]{1,2,0:T(8,128)(2,1)}) async-done(((bf16[8,16,3,512]{3,1,2,0:T(8,128)(2,1)}, bf16[8,512,16]{1,2,0:T(8,128)(2,1)}, bf16[8,16,2048]{2,1,0:T(8,128)(2,1)}, bf16[8,2048,16]{1,2,0:T(8,128)(2,1)}), (bf16[8,16,3,512]{3,1,2,0:T(8,128)(2,1)}, ...) | async-done | bytes 1572880 | tf_op jit(solution)/shard_map/psum | solution.py:322
  2311.1 101.4 %reduce-scatter.16.cloned.1.call-done = f32[1024,1024]{1,0:T(8,128)} async-done(((f32[2048,1024]{1,0:T(8,128)}), f32[1024,1024]{1,0:T(8,128)}) %reduce-scatter.16.cloned.1.call-update) | async-done | bytes 4194320 | tf_op jit(solution)/shard_map/reduce_scatter | solution.py:137
  2418.1 136.9 %all-reduce.5.cloned.1.call-done = (f32[8,1024,16]{1,2,0:T(8,128)}, f32[8,16,1024]{2,1,0:T(8,128)}, f32[8,1024,16]{1,2,0:T(8,128)}, f32[8,16,1024]{2,1,0:T(8,128)}) async-done(((f32[8,1024,16]{1,2,0:T(8,128)}, f32[8,16,1024]{2,1,0:T(8,128)}, f32[8,1024,16]{1,2,0:T(8,128)}, f32[8,16,1024]{2,1,0:T(8,128)}), (f32[8,1024,16]{1,2,0:T(8,128)}, f32[8,16,1024]{2,1,0:T(8,128)}, f32[8,1024,16]{1,2,0:T(8,128)}, ...) | async-done | bytes 2097168 | tf_op jit(solution)/shard_map/psum | solution.py:329
  (424 shorter events, 1147.3 us)
Async XLA Ops:
  14.5 316.5 %all-gather.35.cloned.1.call-start = ((), (), s32[]{:S(2)}) async-start(), calls=%async_computation.25 | async-start | bytes 1114112 | tf_op jit(solution)/shard_map/all_gather | solution.py:124
  15.3 326.3 %reduce-scatter.22.cloned.1.call-start = ((), (), s32[]{:S(2)}) async-start(), calls=%async_computation.27 | async-start | bytes 196608 | tf_op jit(solution)/shard_map/reduce_scatter | solution.py:138
  331.0 112.0 %reduce-scatter.20.cloned.1.call-start = ((), (), s32[]{:S(2)}) async-start(), calls=%async_computation.26 | async-start | bytes 12582912 | tf_op jit(solution)/shard_map/reduce_scatter | solution.py:137
  338.6 157.3 %all-gather.39.cloned.1.call-start = ((), (), s32[]{:S(2)}) async-start(), calls=%async_computation.29 | async-start | bytes 4456448 | tf_op jit(solution)/shard_map/all_gather | solution.py:123
  339.2 213.6 %all-gather.37.cloned.1.call-start = ((), (), s32[]{:S(2)}) async-start(), calls=%async_computation.28 | async-start | bytes 6291456 | tf_op jit(solution)/shard_map/all_gather | solution.py:130
  450.1 161.1 %all-gather.29.cloned.1.call-start = ((), (), s32[]{:S(2)}) async-start(), calls=%async_computation.22 | async-start | bytes 6291456 | tf_op jit(solution)/shard_map/all_gather | solution.py:144
  450.9 213.3 %all-gather.27.cloned.1.call-start = ((), (), s32[]{:S(2)}) async-start(), calls=%async_computation.21 | async-start | bytes 4456448 | tf_op jit(solution)/shard_map/all_gather | solution.py:124
  451.6 258.2 %reduce-scatter.26.cloned.1.call-start = ((), (), s32[]{:S(2)}) async-start(), calls=%async_computation.31 | async-start | bytes 196608 | tf_op jit(solution)/shard_map/reduce_scatter | solution.py:152
  695.1 112.6 %reduce-scatter.24.cloned.1.call-start = ((), (), s32[]{:S(2)}) async-start(), calls=%async_computation.30 | async-start | bytes 12582912 | tf_op jit(solution)/shard_map/reduce_scatter | solution.py:151
  709.7 165.1 %all-gather.41.cloned.1.call-start = ((), (), s32[]{:S(2)}) async-start(), calls=%async_computation.32 | async-start | bytes 6291456 | tf_op jit(solution)/shard_map/all_gather | solution.py:144
  818.0 727.5 %reduce-scatter.30.cloned.1.call-start = ((), (), s32[]{:S(2)}) async-start(), calls=%async_computation.34 | async-start | bytes 196608 | tf_op jit(solution)/shard_map/reduce_scatter | solution.py:152
  1543.5 147.4 %all-gather.17.cloned.1.call-start = ((), (), s32[]{:S(2)}) async-start(), calls=%async_computation.12 | async-start | bytes 3342336 | tf_op jit(solution)/shard_map/all_gather | solution.py:123
  1544.1 204.6 %all-gather.15.cloned.1.call-start = ((), (), s32[]{:S(2)}) async-start(), calls=%async_computation.11 | async-start | bytes 6291456 | tf_op jit(solution)/shard_map/all_gather | solution.py:130
  1654.0 257.9 %all-gather.19.cloned.1.call-start = ((), (), s32[]{:S(2)}) async-start(), calls=%async_computation.13 | async-start | bytes 1114112 | tf_op jit(solution)/shard_map/all_gather | solution.py:124
  1654.6 267.6 %reduce-scatter.14.cloned.1.call-start = ((), (), s32[]{:S(2)}) async-start(), calls=%async_computation.15 | async-start | bytes 196608 | tf_op jit(solution)/shard_map/reduce_scatter | solution.py:138
  1911.9 112.0 %reduce-scatter.12.cloned.1.call-start = ((), (), s32[]{:S(2)}) async-start(), calls=%async_computation.14 | async-start | bytes 12582912 | tf_op jit(solution)/shard_map/reduce_scatter | solution.py:137
  1919.5 157.0 %all-gather.23.cloned.1.call-start = ((), (), s32[]{:S(2)}) async-start(), calls=%async_computation.17 | async-start | bytes 4456448 | tf_op jit(solution)/shard_map/all_gather | solution.py:123
  1920.1 213.8 %all-gather.21.cloned.1.call-start = ((), (), s32[]{:S(2)}) async-start(), calls=%async_computation.16 | async-start | bytes 6291456 | tf_op jit(solution)/shard_map/all_gather | solution.py:130
  2031.0 155.8 %all-gather.25.cloned.1.call-start = ((), (), s32[]{:S(2)}) async-start(), calls=%async_computation.18 | async-start | bytes 4456448 | tf_op jit(solution)/shard_map/all_gather | solution.py:124
  2031.8 169.7 %reduce-scatter.32.cloned.1.call-start = ((), (), s32[]{:S(2)}) async-start(), calls=%async_computation.35 | async-start | bytes 196608 | tf_op jit(solution)/shard_map/reduce_scatter | solution.py:138
  2050.0 249.2 %all-reduce.7.cloned.1.call-start = ((), (), s32[]{:S(2)}) async-start(), calls=%async_computation.37 | async-start | bytes 3145728 | tf_op jit(solution)/shard_map/psum | solution.py:322
  2058.6 252.5 %reduce-scatter.18.cloned.1.call-start = ((), (), s32[]{:S(2)}) async-start(), calls=%async_computation.20 | async-start | bytes 196608 | tf_op jit(solution)/shard_map/reduce_scatter | solution.py:138
  2165.7 246.9 %reduce-scatter.16.cloned.1.call-start = ((), (), s32[]{:S(2)}) async-start(), calls=%async_computation.19 | async-start | bytes 12582912 | tf_op jit(solution)/shard_map/reduce_scatter | solution.py:137
  2201.4 353.7 %all-reduce.5.cloned.1.call-start = ((), (), s32[]{:S(2)}) async-start(), calls=%async_computation.36 | async-start | bytes 4194304 | tf_op jit(solution)/shard_map/psum | solution.py:329
  (52 other events, 1761.5 us)
Sparse Core Ops, SparseCore 0:
  10.2 48.1 all-gather.32
  60.0 55.5 all-gather.30
  117.7 37.9 all-gather.34
  331.1 10.3 reduce-scatter.21
  343.7 99.2 reduce-scatter.19
  445.2 50.6 all-gather.38
  497.6 55.2 all-gather.36
  554.5 56.7 all-gather.28
  613.6 50.5 all-gather.26
  709.9 97.7 reduce-scatter.23
  818.1 56.7 all-gather.40
  1531.7 10.2 reduce-scatter.29
  1544.2 99.2 reduce-scatter.27
  1645.7 45.1 all-gather.16
  1693.0 55.6 all-gather.14
  1750.9 37.8 all-gather.18
  1912.0 10.1 reduce-scatter.13
  1924.6 99.2 reduce-scatter.11
  2025.8 50.6 all-gather.22
  2078.6 55.1 all-gather.20
  2136.0 50.7 all-gather.24
  2203.1 96.0 all-reduce.6
  2313.3 99.2 reduce-scatter.15
  2420.2 134.7 all-reduce.4
  (3 shorter events, 26.4 us)
where the time goes:
time: 2580 us; the launch traced here: 2570 us
  waiting for transfers between devices  1200 us (47%)
  matrix products  1030 us (40%)
  local copies, waits for them, and re-layouts  148 us (6%)
  other arithmetic  123 us (5%)
  blocking collectives  28.7 us (1%)
    reduce_scatter x3, waiting for transfers between devices, leave_rows(): lax.psum_scatter(partial_value, 'tensor', scatter_dimension=0, tiled=True)  305 us
    all_gather x4, waiting for transfers between devices, enter_rows(): lax.all_gather(normed, 'tensor', axis=0, tiled=True)  214 us
    reduce_scatter x2, waiting for transfers between devices, leave_grads(): lax.psum_scatter(partial_value, 'tensor', scatter_dimension=0, tiled=True)  196 us
    dot_general x4, matrix products, one_block(): jnp.einsum('hqk,qhd->khd', slopes, query_block, preferred_element_type=jn...  177 us
    dot_general x4, matrix products, one_block(): jnp.einsum('hqk,khd->qhd', slopes, key_rows, preferred_element_type=jnp.f...  170 us
    dot_general x22, matrix products, matmul(): return jnp.dot(left, right, preferred_element_type=jnp.float32)  141 us
    psum x1, waiting for transfers between devices, per_device(): lax.psum((spread(grad_a_qkv_here, 0), spread(grad_b_out_here, 1), spread(...  137 us
    dot_general x8, matrix products, masked_scores(): jnp.einsum('qhd,khd->hqk', query_block, key_rows, preferred_element_type=...  129 us
  transfers between devices with their start and end apart: 27, of which 22 were waited for; matrix products, arithmetic and copies ran while one was open for 23% of the time, Pallas kernels for 0%

commit v1 on v0

--- a/solution.py
+++ b/solution.py
@@ -327,13 +327,16 @@
         lax.psum(spread(grad_a_down_here, 3).astype(jnp.bfloat16), "dp").astype(jnp.float32),
     )
     shared = lax.psum(
-        (
-            spread(grad_a_qkv_here, 0),
-            spread(grad_b_out_here, 1),
-            spread(grad_a_up_here, 2),
-            spread(grad_b_down_here, 3),
+        lax.psum(
+            (
+                spread(grad_a_qkv_here, 0),
+                spread(grad_b_out_here, 1),
+                spread(grad_a_up_here, 2),
+                spread(grad_b_down_here, 3),
+            ),
+            "tensor",
         ),
-        ("dp", "tensor"),
+        "dp",
     )
     return (
         output.astype(jnp.bfloat16),

time: 2580 us -> 2610 us (1.012)
  waiting for transfers between devices: 1200 us -> 1230 us
    psum x0 -> x1, waiting for transfers between devices: none -> 96.7 us  [per_device(): lax.psum(lax.psum((spread(grad_a_qkv_here, 0), spread(grad_b_out_here, 1)...]
    psum x1, waiting for transfers between devices: 137 us -> 50.8 us  [per_device(): lax.psum((spread(grad_a_qkv_here, 0), spread(grad_b_out_here, 1), spread(...]
  transfers between devices with their start and end apart: 27 -> 28, of which waited for: 22 -> 22; matrix products, arithmetic and copies ran while one was open for 23% -> 23% of each run, Pallas kernels for 0% -> 0%
where the time goes in v1:
time: 2610 us; the launch traced here: 2600 us
  waiting for transfers between devices  1230 us (47%)
  matrix products  1030 us (39%)
  local copies, waits for them, and re-layouts  147 us (6%)
  other arithmetic  123 us (5%)
  blocking collectives  28.7 us (1%)
    reduce_scatter x3, waiting for transfers between devices, leave_rows(): lax.psum_scatter(partial_value, 'tensor', scatter_dimension=0, tiled=True)  300 us
    all_gather x4, waiting for transfers between devices, enter_rows(): lax.all_gather(normed, 'tensor', axis=0, tiled=True)  214 us
    reduce_scatter x2, waiting for transfers between devices, leave_grads(): lax.psum_scatter(partial_value, 'tensor', scatter_dimension=0, tiled=True)  196 us
    dot_general x4, matrix products, one_block(): jnp.einsum('hqk,qhd->khd', slopes, query_block, preferred_element_type=jn...  177 us
    dot_general x4, matrix products, one_block(): jnp.einsum('hqk,khd->qhd', slopes, key_rows, preferred_element_type=jnp.f...  170 us
    dot_general x22, matrix products, matmul(): return jnp.dot(left, right, preferred_element_type=jnp.float32)  141 us
    dot_general x8, matrix products, masked_scores(): jnp.einsum('qhd,khd->hqk', query_block, key_rows, preferred_element_type=...  129 us
    dot_general x8, matrix products, one_block(): jnp.einsum('hqk,khd->qhd', weights_low, value_rows, preferred_element_typ...  115 us
  transfers between devices with their start and end apart: 28, of which 22 were waited for; matrix products, arithmetic and copies ran while one was open for 23% of the time, Pallas kernels for 0%

profile of v1, /device:TPU:0, one launch (start us, length us, event | category | flops | bytes accessed | tf_op | source)
XLA Modules:
  0.0 2596.2 jit_solution(559693052840409561)
XLA Ops:
  62.9 52.5 %all-gather.31.cloned.1.call-done = bf16[2048,1024]{1,0:T(8,128)(2,1)} async-done(((bf16[1024,1024]{1,0:T(8,128)(2,1)}), bf16[2048,1024]{1,0:T(8,128)(2,1)}) %all-gather.31.cloned.1.call-update) | async-done | bytes 4194320 | tf_op jit(solution)/shard_map/all_gather | solution.py:130
  131.0 196.6 %while.38 = (s32[]{:T(128)}, bf16[4,512,512]{2,1,0:T(8,128)(2,1)}, f32[4,8,512]{2,1,0:T(8,128)S(1)}, s32[4]{0:T(128)S(1)}, s32[1,2]{1,0:T(1,128)S(1)}, /*index=5...) while((s32[]{:T(128)}, bf16[4,512,512]{2,1,0:T(8,128)(2,1)}, ...), condition=%wide.region_21.22_spmd, body=%wide.region_16.21_spmd.sunk | while | flops 2252623360 | bytes 112358664 | solution.py:78
  341.0 101.4 %reduce-scatter.20.cloned.1.call-done = f32[1024,1024]{1,0:T(8,128)} async-done(((f32[2048,1024]{1,0:T(8,128)}), f32[1024,1024]{1,0:T(8,128)}) %reduce-scatter.20.cloned.1.call-update) | async-done | bytes 4194320 | tf_op jit(solution)/shard_map/reduce_scatter | solution.py:137
  495.4 56.9 %all-gather.37.cloned.1.call-done = bf16[2048,1024]{1,0:T(8,128)(2,1)} async-done(((bf16[1024,1024]{1,0:T(8,128)(2,1)}), bf16[2048,1024]{1,0:T(8,128)(2,1)}) %all-gather.37.cloned.1.call-update) | async-done | bytes 4194320 | tf_op jit(solution)/shard_map/all_gather | solution.py:130
  610.7 53.0 %all-gather.27.cloned.1.call-done = bf16[2048,1024]{0,1:T(8,128)(2,1)} async-done(((bf16[2048,64]{0,1:T(8,128)(2,1)}), bf16[2048,1024]{0,1:T(8,128)(2,1)}) %all-gather.27.cloned.1.call-update) | async-done | bytes 4194320 | tf_op jit(solution)/shard_map/all_gather | solution.py:124
  709.0 97.8 %reduce-scatter.24.cloned.1.call-done = f32[1024,1024]{1,0:T(8,128)} async-done(((f32[2048,1024]{1,0:T(8,128)}), f32[1024,1024]{1,0:T(8,128)}) %reduce-scatter.24.cloned.1.call-update) | async-done | bytes 4194320 | tf_op jit(solution)/shard_map/reduce_scatter | solution.py:151
  824.2 49.9 %all-gather.41.cloned.1.call-done = bf16[2048,1024]{1,0:T(8,128)(2,1)} async-done(((bf16[1024,1024]{1,0:T(8,128)(2,1)}), bf16[2048,1024]{1,0:T(8,128)(2,1)}) %all-gather.41.cloned.1.call-update) | async-done | bytes 4194320 | tf_op jit(solution)/shard_map/all_gather | solution.py:144
  881.9 636.6 %while.39 = (s32[]{:T(128)}, f32[2048,8,64]{0,2,1:T(8,128)}, f32[2048,8,64]{0,2,1:T(8,128)}, bf16[4,512,8,64]{1,0,3,2:T(4,128)(2,1)}, s32[4]{0:T(128)S(1)}, /*in...) while((s32[]{:T(128)}, f32[2048,8,64]{0,2,1:T(8,128)}, ...), condition=%wide.region_34.35_spmd.clone, body=%wide.region_30.34_spmd.clone.sunk | while | flops 5494574592 | bytes 331953440 | solution.py:115
  932.1 42.6 %fusion.336 = bf16[1,512,8,64]{1,3,2,0:T(8,128)(2,1)S(1)} fusion(bf16[2048,8,64]{0,2,1:T(8,128)(2,1)} %get-tuple-element.554, f32[8,512,2048]{2,1,0:T(8,128)} %subtract_exponential_fusion.4, f32[8,512,2048]{2,1,0:T(8,128)} %fusion.335), kind=kOutput, calls=%fused_computation.66.clone.1 | convolution fusion | flops 1115691008 | bytes 69730304 | tf_op jit(solution)/shard_map/while/body/eval_jaxpr/hqk,khd->qhd/dot_general | solution.py:99
  974.7 43.4 %bitcast_add_fusion.5 = f32[2048,8,64]{0,2,1:T(8,128)} fusion(f32[2048,8,64]{0,2,1:T(8,128)} %get-tuple-element.533, f32[8,512,2048]{2,1,0:T(8,128)} %subtract_exponential_fusion.4, f32[8,512,2048]{2,1,0:T(8,128)} %fusion.335, pred[]{:T(512)S(6)} %compare.3, bf16[2048,8,64]{0,2,1:T(8,128)(2,1)} %get-tuple-element.552, s32[]{:T(128)S(6)} %select_n.138), kind=kOutput, calls=%fused_computation.63.clone.1 | convolution fusion | flops 1117788160 | bytes 143130624 | tf_op jit(solution)/shard_map/while/body/eval_jaxpr/hqk,qhd->khd/dot_general | solution.py:102
  1090.5 42.6 %fusion.336 = bf16[1,512,8,64]{1,3,2,0:T(8,128)(2,1)S(1)} fusion(bf16[2048,8,64]{0,2,1:T(8,128)(2,1)} %get-tuple-element.554, f32[8,512,2048]{2,1,0:T(8,128)} %subtract_exponential_fusion.4, f32[8,512,2048]{2,1,0:T(8,128)} %fusion.335), kind=kOutput, calls=%fused_computation.66.clone.1 | convolution fusion | flops 1115691008 | bytes 69730304 | tf_op jit(solution)/shard_map/while/body/eval_jaxpr/hqk,khd->qhd/dot_general | solution.py:99
  1133.1 44.6 %bitcast_add_fusion.5 = f32[2048,8,64]{0,2,1:T(8,128)} fusion(f32[2048,8,64]{0,2,1:T(8,128)} %get-tuple-element.533, f32[8,512,2048]{2,1,0:T(8,128)} %subtract_exponential_fusion.4, f32[8,512,2048]{2,1,0:T(8,128)} %fusion.335, pred[]{:T(512)S(6)} %compare.3, bf16[2048,8,64]{0,2,1:T(8,128)(2,1)} %get-tuple-element.552, s32[]{:T(128)S(6)} %select_n.138), kind=kOutput, calls=%fused_computation.63.clone.1 | convolution fusion | flops 1117788160 | bytes 143130624 | tf_op jit(solution)/shard_map/while/body/eval_jaxpr/hqk,qhd->khd/dot_general | solution.py:102
  1292.7 44.6 %bitcast_add_fusion.5 = f32[2048,8,64]{0,2,1:T(8,128)} fusion(f32[2048,8,64]{0,2,1:T(8,128)} %get-tuple-element.533, f32[8,512,2048]{2,1,0:T(8,128)} %subtract_exponential_fusion.4, f32[8,512,2048]{2,1,0:T(8,128)} %fusion.335, pred[]{:T(512)S(6)} %compare.3, bf16[2048,8,64]{0,2,1:T(8,128)(2,1)} %get-tuple-element.552, s32[]{:T(128)S(6)} %select_n.138), kind=kOutput, calls=%fused_computation.63.clone.1 | convolution fusion | flops 1117788160 | bytes 143130624 | tf_op jit(solution)/shard_map/while/body/eval_jaxpr/hqk,qhd->khd/dot_general | solution.py:102
  1409.8 42.6 %fusion.336 = bf16[1,512,8,64]{1,3,2,0:T(8,128)(2,1)S(1)} fusion(bf16[2048,8,64]{0,2,1:T(8,128)(2,1)} %get-tuple-element.554, f32[8,512,2048]{2,1,0:T(8,128)} %subtract_exponential_fusion.4, f32[8,512,2048]{2,1,0:T(8,128)} %fusion.335), kind=kOutput, calls=%fused_computation.66.clone.1 | convolution fusion | flops 1115691008 | bytes 69730304 | tf_op jit(solution)/shard_map/while/body/eval_jaxpr/hqk,khd->qhd/dot_general | solution.py:99
  1452.4 44.6 %bitcast_add_fusion.5 = f32[2048,8,64]{0,2,1:T(8,128)} fusion(f32[2048,8,64]{0,2,1:T(8,128)} %get-tuple-element.533, f32[8,512,2048]{2,1,0:T(8,128)} %subtract_exponential_fusion.4, f32[8,512,2048]{2,1,0:T(8,128)} %fusion.335, pred[]{:T(512)S(6)} %compare.3, bf16[2048,8,64]{0,2,1:T(8,128)(2,1)} %get-tuple-element.552, s32[]{:T(128)S(6)} %select_n.138), kind=kOutput, calls=%fused_computation.63.clone.1 | convolution fusion | flops 1117788160 | bytes 143130624 | tf_op jit(solution)/shard_map/while/body/eval_jaxpr/hqk,qhd->khd/dot_general | solution.py:102
  1544.4 98.0 %reduce-scatter.28.cloned.1.call-done = f32[1024,1024]{1,0:T(8,128)} async-done(((f32[2048,1024]{1,0:T(8,128)}), f32[1024,1024]{1,0:T(8,128)}) %reduce-scatter.28.cloned.1.call-update) | async-done | bytes 4194320 | tf_op jit(solution)/shard_map/reduce_scatter | solution.py:151
  1700.5 47.1 %all-gather.15.cloned.1.call-done = bf16[2048,1024]{1,0:T(8,128)(2,1)} async-done(((bf16[1024,1024]{1,0:T(8,128)(2,1)}), bf16[2048,1024]{1,0:T(8,128)(2,1)}) %all-gather.15.cloned.1.call-update) | async-done | bytes 4194320 | tf_op jit(solution)/shard_map/all_gather | solution.py:130
  1763.2 144.9 %while.37 = (s32[]{:T(128)}, bf16[4,512,512]{2,1,0:T(8,128)(2,1)}, s32[4]{0:T(128)S(1)}, s32[1,2]{1,0:T(1,128)S(1)}, bf16[2048,8,64]{0,2,1:T(8,128)(2,1)}, /*ind...) while((s32[]{:T(128)}, bf16[4,512,512]{2,1,0:T(8,128)(2,1)}, ...), condition=%wide.region_7.8_spmd, body=%wide.region_2.7_spmd.sunk | while | flops 2202297856 | bytes 76608768 | solution.py:78
  1926.1 96.8 %reduce-scatter.12.cloned.1.call-done = f32[1024,1024]{1,0:T(8,128)} async-done(((f32[2048,1024]{1,0:T(8,128)}), f32[1024,1024]{1,0:T(8,128)}) %reduce-scatter.12.cloned.1.call-update) | async-done | bytes 4194320 | tf_op jit(solution)/shard_map/reduce_scatter | solution.py:137
  2088.8 57.4 %all-gather.21.cloned.1.call-done = bf16[2048,1024]{1,0:T(8,128)(2,1)} async-done(((bf16[1024,1024]{1,0:T(8,128)(2,1)}), bf16[2048,1024]{1,0:T(8,128)(2,1)}) %all-gather.21.cloned.1.call-update) | async-done | bytes 4194320 | tf_op jit(solution)/shard_map/all_gather | solution.py:130
  2213.7 50.8 %all-reduce.9.cloned.1.call-done = (f32[8,1024,16]{1,2,0:T(8,128)}, f32[8,16,1024]{2,1,0:T(8,128)}, f32[8,1024,16]{1,2,0:T(8,128)}, f32[8,16,1024]{2,1,0:T(8,128)}) async-done(((f32[8,1024,16]{1,2,0:T(8,128)}, f32[8,16,1024]{2,1,0:T(8,128)}, f32[8,1024,16]{1,2,0:T(8,128)}, f32[8,16,1024]{2,1,0:T(8,128)}), (f32[8,1024,16]{1,2,0:T(8,128)}, f32[8,16,1024]{2,1,0:T(8,128)}, f32[8,1024,16]{1,2,0:T(8,128)}, ...) | async-done | bytes 2097168 | tf_op jit(solution)/shard_map/psum | solution.py:330
  2264.6 101.4 %all-reduce.11.cloned.1.call-done = (bf16[8,16,3,512]{3,1,2,0:T(8,128)(2,1)}, bf16[8,512,16]{1,2,0:T(8,128)(2,1)}, bf16[8,16,2048]{2,1,0:T(8,128)(2,1)}, bf16[8,2048,16]{1,2,0:T(8,128)(2,1)}) async-done(((bf16[8,16,3,512]{3,1,2,0:T(8,128)(2,1)}, bf16[8,512,16]{1,2,0:T(8,128)(2,1)}, bf16[8,16,2048]{2,1,0:T(8,128)(2,1)}, bf16[8,2048,16]{1,2,0:T(8,128)(2,1)}), (bf16[8,16,3,512]{3,1,2,0:T(8,128)(2,1)}, ...) | async-done | bytes 1572880 | tf_op jit(solution)/shard_map/psum | solution.py:322
  2377.8 101.5 %reduce-scatter.16.cloned.1.call-done = f32[1024,1024]{1,0:T(8,128)} async-done(((f32[2048,1024]{1,0:T(8,128)}), f32[1024,1024]{1,0:T(8,128)}) %reduce-scatter.16.cloned.1.call-update) | async-done | bytes 4194320 | tf_op jit(solution)/shard_map/reduce_scatter | solution.py:137
  2484.9 96.7 %all-reduce.7.cloned.1.call-done = (f32[8,1024,16]{1,2,0:T(8,128)}, f32[8,16,1024]{2,1,0:T(8,128)}, f32[8,1024,16]{1,2,0:T(8,128)}, f32[8,16,1024]{2,1,0:T(8,128)}) async-done(((f32[8,1024,16]{1,2,0:T(8,128)}, f32[8,16,1024]{2,1,0:T(8,128)}, f32[8,1024,16]{1,2,0:T(8,128)}, f32[8,16,1024]{2,1,0:T(8,128)}), (f32[8,1024,16]{1,2,0:T(8,128)}, f32[8,16,1024]{2,1,0:T(8,128)}, f32[8,1024,16]{1,2,0:T(8,128)}, ...) | async-done | bytes 2097168 | tf_op jit(solution)/shard_map/psum | solution.py:329
  (427 shorter events, 1197.4 us)
Async XLA Ops:
  14.5 316.0 %all-gather.35.cloned.1.call-start = ((), (), s32[]{:S(2)}) async-start(), calls=%async_computation.25 | async-start | bytes 1114112 | tf_op jit(solution)/shard_map/all_gather | solution.py:124
  15.3 325.7 %reduce-scatter.22.cloned.1.call-start = ((), (), s32[]{:S(2)}) async-start(), calls=%async_computation.27 | async-start | bytes 196608 | tf_op jit(solution)/shard_map/reduce_scatter | solution.py:138
  338.1 157.3 %all-gather.39.cloned.1.call-start = ((), (), s32[]{:S(2)}) async-start(), calls=%async_computation.29 | async-start | bytes 4456448 | tf_op jit(solution)/shard_map/all_gather | solution.py:123
  338.7 213.6 %all-gather.37.cloned.1.call-start = ((), (), s32[]{:S(2)}) async-start(), calls=%async_computation.28 | async-start | bytes 6291456 | tf_op jit(solution)/shard_map/all_gather | solution.py:130
  449.6 161.1 %all-gather.29.cloned.1.call-start = ((), (), s32[]{:S(2)}) async-start(), calls=%async_computation.22 | async-start | bytes 6291456 | tf_op jit(solution)/shard_map/all_gather | solution.py:144
  450.3 213.3 %all-gather.27.cloned.1.call-start = ((), (), s32[]{:S(2)}) async-start(), calls=%async_computation.21 | async-start | bytes 4456448 | tf_op jit(solution)/shard_map/all_gather | solution.py:124
  451.1 258.0 %reduce-scatter.26.cloned.1.call-start = ((), (), s32[]{:S(2)}) async-start(), calls=%async_computation.31 | async-start | bytes 196608 | tf_op jit(solution)/shard_map/reduce_scatter | solution.py:152
  694.3 112.5 %reduce-scatter.24.cloned.1.call-start = ((), (), s32[]{:S(2)}) async-start(), calls=%async_computation.30 | async-start | bytes 12582912 | tf_op jit(solution)/shard_map/reduce_scatter | solution.py:151
  709.0 165.2 %all-gather.41.cloned.1.call-start = ((), (), s32[]{:S(2)}) async-start(), calls=%async_computation.32 | async-start | bytes 6291456 | tf_op jit(solution)/shard_map/all_gather | solution.py:144
  817.2 727.2 %reduce-scatter.30.cloned.1.call-start = ((), (), s32[]{:S(2)}) async-start(), calls=%async_computation.34 | async-start | bytes 196608 | tf_op jit(solution)/shard_map/reduce_scatter | solution.py:152
  1542.5 147.4 %all-gather.17.cloned.1.call-start = ((), (), s32[]{:S(2)}) async-start(), calls=%async_computation.12 | async-start | bytes 3342336 | tf_op jit(solution)/shard_map/all_gather | solution.py:123
  1543.0 204.5 %all-gather.15.cloned.1.call-start = ((), (), s32[]{:S(2)}) async-start(), calls=%async_computation.11 | async-start | bytes 6291456 | tf_op jit(solution)/shard_map/all_gather | solution.py:130
  1652.9 258.1 %all-gather.19.cloned.1.call-start = ((), (), s32[]{:S(2)}) async-start(), calls=%async_computation.13 | async-start | bytes 1114112 | tf_op jit(solution)/shard_map/all_gather | solution.py:124
  1653.5 272.6 %reduce-scatter.14.cloned.1.call-start = ((), (), s32[]{:S(2)}) async-start(), calls=%async_computation.15 | async-start | bytes 196608 | tf_op jit(solution)/shard_map/reduce_scatter | solution.py:138
  1911.0 112.0 %reduce-scatter.12.cloned.1.call-start = ((), (), s32[]{:S(2)}) async-start(), calls=%async_computation.14 | async-start | bytes 12582912 | tf_op jit(solution)/shard_map/reduce_scatter | solution.py:137
  1918.6 124.3 %reduce-scatter.32.cloned.1.call-start = ((), (), s32[]{:S(2)}) async-start(), calls=%async_computation.35 | async-start | bytes 196608 | tf_op jit(solution)/shard_map/reduce_scatter | solution.py:138
  1925.3 163.4 %all-gather.23.cloned.1.call-start = ((), (), s32[]{:S(2)}) async-start(), calls=%async_computation.17 | async-start | bytes 4456448 | tf_op jit(solution)/shard_map/all_gather | solution.py:123
  1926.1 220.1 %all-gather.21.cloned.1.call-start = ((), (), s32[]{:S(2)}) async-start(), calls=%async_computation.16 | async-start | bytes 6291456 | tf_op jit(solution)/shard_map/all_gather | solution.py:130
  2030.1 169.0 %all-gather.25.cloned.1.call-start = ((), (), s32[]{:S(2)}) async-start(), calls=%async_computation.18 | async-start | bytes 4456448 | tf_op jit(solution)/shard_map/all_gather | solution.py:124
  2030.8 233.7 %all-reduce.9.cloned.1.call-start = ((), (), s32[]{:S(2)}) async-start(), calls=%async_computation.37 | async-start | bytes 4194304 | tf_op jit(solution)/shard_map/psum | solution.py:330
  2050.7 315.2 %all-reduce.11.cloned.1.call-start = ((), (), s32[]{:S(2)}) async-start(), calls=%async_computation.38 | async-start | bytes 3145728 | tf_op jit(solution)/shard_map/psum | solution.py:322
  2059.4 318.4 %reduce-scatter.18.cloned.1.call-start = ((), (), s32[]{:S(2)}) async-start(), calls=%async_computation.20 | async-start | bytes 196608 | tf_op jit(solution)/shard_map/reduce_scatter | solution.py:138
  2178.0 301.3 %reduce-scatter.16.cloned.1.call-start = ((), (), s32[]{:S(2)}) async-start(), calls=%async_computation.19 | async-start | bytes 12582912 | tf_op jit(solution)/shard_map/reduce_scatter | solution.py:137
  2213.7 367.9 %all-reduce.7.cloned.1.call-start = ((), (), s32[]{:S(2)}) async-start(), calls=%async_computation.36 | async-start | bytes 4194304 | tf_op jit(solution)/shard_map/psum | solution.py:329
  (53 other events, 1866.4 us)
Sparse Core Ops, SparseCore 0:
  10.2 47.8 all-gather.32
  59.7 55.5 all-gather.30
  117.5 37.9 all-gather.34
  330.6 10.3 reduce-scatter.21
  343.1 99.2 reduce-scatter.19
  444.7 50.7 all-gather.38
  497.0 55.2 all-gather.36
  553.9 56.7 all-gather.28
  613.1 50.5 all-gather.26
  709.1 97.7 reduce-scatter.23
  817.3 56.7 all-gather.40
  1530.6 10.2 reduce-scatter.29
  1543.1 99.2 reduce-scatter.27
  1644.6 45.2 all-gather.16
  1691.9 55.6 all-gather.14
  1749.8 37.8 all-gather.18
  1923.6 99.2 reduce-scatter.11
  2038.0 50.6 all-gather.22
  2090.9 55.2 all-gather.20
  2148.3 50.7 all-gather.24
  2202.5 61.9 all-reduce.8
  2270.0 95.9 all-reduce.10
  2380.0 99.2 reduce-scatter.15
  2483.2 98.2 all-reduce.6
  (4 shorter events, 38.0 us)
